TPU v7x, 32 devices: a whole 2x2x4 slice. The times are simulated.
32 devices in a mesh: dp: 8 (over z, y), seq: 4 (over x, core).
Axes of the slice: x: 2, y: 2, z: 4, core: 2. Of those that a mesh axis runs over, the one named last changes fastest.
Arguments:
- inputs: bfloat16 [16, 1024, 768], P('dp', 'seq'), may hold values from -6 to 6
- lengths: int32 [16], P('dp'), may hold values from 512 to 1024, as said below
- query_weight: bfloat16 [768, 768], P('dp'), may hold values from -0.3125 to 0.3125
- key_weight: bfloat16 [768, 768], P('dp'), may hold values from -0.3125 to 0.3125
- value_weight: bfloat16 [768, 768], P('dp'), may hold values from -0.21875 to 0.21875
- output_weight: bfloat16 [768, 768], P('dp'), may hold values from -0.625 to 0.625
- up_weight: bfloat16 [768, 3072], P('dp'), may hold values from -0.21875 to 0.21875
- down_weight: bfloat16 [3072, 768], P('dp'), may hold values from -0.15625 to 0.15625
- query_bias: bfloat16 [768], P('dp'), may hold values from -3 to 3
- value_bias: bfloat16 [768], P('dp'), may hold values from -3 to 3
- output_bias: bfloat16 [768], P('dp'), may hold values from -3 to 3
- up_bias: bfloat16 [3072], P('dp'), may hold values from -3 to 3
- down_bias: bfloat16 [768], P('dp'), may hold values from -3 to 3
- first_gain: bfloat16 [768], P('dp'), may hold values from 0.5 to 1.5
- first_shift: bfloat16 [768], P('dp'), may hold values from -2 to 2
- second_gain: bfloat16 [768], P('dp'), may hold values from 0.5 to 1.5
- second_shift: bfloat16 [768], P('dp'), may hold values from -2 to 2
- cotangent: bfloat16 [16, 1024, 768], P('dp', 'seq'), may hold values from -6 to 6
Outputs:
- layer_out: bfloat16 [16, 1024, 768], P('dp', 'seq')
- input_grad: bfloat16 [16, 1024, 768], P('dp', 'seq')
- query_weight_grad: float32 [768, 768], P('dp')
- key_weight_grad: float32 [768, 768], P('dp')
- value_weight_grad: float32 [768, 768], P('dp')
- output_weight_grad: float32 [768, 768], P('dp')
- up_weight_grad: float32 [768, 3072], P('dp')
- down_weight_grad: float32 [3072, 768], P('dp')
- query_bias_grad: float32 [768], P('dp')
- value_bias_grad: float32 [768], P('dp')
- output_bias_grad: float32 [768], P('dp')
- up_bias_grad: float32 [3072], P('dp')
- down_bias_grad: float32 [768], P('dp')
- first_gain_grad: float32 [768], P('dp')
- first_shift_grad: float32 [768], P('dp')
- second_gain_grad: float32 [768], P('dp')
- second_shift_grad: float32 [768], P('dp')
Inputs may be any that keep to these rules, and one draw needn't show every extreme that they name: `lengths`: the number of real tokens of each sequence; its later positions up to 1024 are padding.
All inputs are finite; a program needn't handle non-finite values.
Results may differ from a plain program's by a relative error of at most 0.015.
Values may be sent and summed in bfloat16 or wider, within the bound.
A program may use at most 192 MiB of HBM per device.

v0:
```python
import jax
import jax.numpy as jnp
from jax import lax
from jax.sharding import PartitionSpec as P

HEAD_DIM = 64
eps_norm = 1e-05
masked_score = -1000000000.0


def layer_norm(hidden, gain_vec, shift_vec):
    row_mean = jnp.mean(hidden, axis=-1, keepdims=True)
    centred = hidden - row_mean
    row_var = jnp.mean(centred * centred, axis=-1, keepdims=True)
    return centred * lax.rsqrt(row_var + eps_norm) * gain_vec + shift_vec


def gelu_exact(pre_act):
    return jax.nn.gelu(pre_act, approximate=False)


def matmul_plain(first_op, second_op):
    return jnp.dot(first_op, second_op, preferred_element_type=jnp.float32)


def inner_rows(first_op, second_op):
    return lax.dot_general(
        first_op, second_op, (((0,), (0,)), ((), ())), preferred_element_type=jnp.float32
    )


def times_transposed(first_op, second_op):
    return lax.dot_general(
        first_op, second_op, (((1,), (1,)), ((), ())), preferred_element_type=jnp.float32
    )


def column_sums(grad_rows):
    return jnp.sum(grad_rows.astype(jnp.float32), axis=0)


def local(
    inputs,
    lengths,
    query_weight,
    key_weight,
    value_weight,
    output_weight,
    up_weight,
    down_weight,
    query_bias,
    value_bias,
    output_bias,
    up_bias,
    down_bias,
    first_gain,
    first_shift,
    second_gain,
    second_shift,
    cotangent,
):
    gathered = (
        lax.all_gather(query_weight, "dp", axis=0, tiled=True),
        lax.all_gather(key_weight, "dp", axis=0, tiled=True),
        lax.all_gather(value_weight, "dp", axis=0, tiled=True),
        lax.all_gather(output_weight, "dp", axis=0, tiled=True),
        lax.all_gather(up_weight, "dp", axis=0, tiled=True),
        lax.all_gather(down_weight, "dp", axis=0, tiled=True),
        lax.all_gather(query_bias, "dp", axis=0, tiled=True),
        lax.all_gather(value_bias, "dp", axis=0, tiled=True),
        lax.all_gather(output_bias, "dp", axis=0, tiled=True),
        lax.all_gather(up_bias, "dp", axis=0, tiled=True),
        lax.all_gather(down_bias, "dp", axis=0, tiled=True),
        lax.all_gather(first_gain, "dp", axis=0, tiled=True),
        lax.all_gather(first_shift, "dp", axis=0, tiled=True),
        lax.all_gather(second_gain, "dp", axis=0, tiled=True),
        lax.all_gather(second_shift, "dp", axis=0, tiled=True),
    )
    full_query, full_key, full_value, full_output, full_up, full_down = gathered[0:6]
    bias_query = gathered[6].astype(jnp.float32)
    bias_value = gathered[7].astype(jnp.float32)
    bias_output = gathered[8].astype(jnp.float32)
    bias_up = gathered[9].astype(jnp.float32)
    bias_down = gathered[10].astype(jnp.float32)
    gain_first = gathered[11].astype(jnp.float32)
    shift_first = gathered[12].astype(jnp.float32)
    gain_second = gathered[13].astype(jnp.float32)
    shift_second = gathered[14].astype(jnp.float32)
    group_count, local_len, model_width = inputs.shape
    row_count = group_count * local_len
    flat_in = inputs.reshape(row_count, model_width)
    queries = (matmul_plain(flat_in, full_query) + bias_query).astype(jnp.bfloat16)
    key_rows = matmul_plain(flat_in, full_key).astype(jnp.bfloat16)
    value_rows = (matmul_plain(flat_in, full_value) + bias_value).astype(jnp.bfloat16)
    stacked = jnp.stack([queries, key_rows, value_rows]).reshape(
        3, group_count, local_len, model_width
    )
    head_layout = lax.all_to_all(stacked, "seq", split_axis=3, concat_axis=2, tiled=True)
    seq_len = head_layout.shape[2]
    head_width = head_layout.shape[3]
    local_heads = head_width // HEAD_DIM
    block_rows = min(512, seq_len)
    block_count = seq_len // block_rows
    score_scale = HEAD_DIM ** (-0.5)

    def attend_forward(operands):
        seq_queries, seq_keys, seq_values, length = operands
        key_heads = seq_keys.reshape(seq_len, local_heads, HEAD_DIM)
        value_heads = seq_values.reshape(seq_len, local_heads, HEAD_DIM)
        key_live = jnp.arange(seq_len) < length

        def one_block(query_block):
            scores = (
                jnp.einsum(
                    "qhd,khd->hqk", query_block, key_heads, preferred_element_type=jnp.float32
                )
                * score_scale
            )
            scores = jnp.where(key_live[None, None, :], scores, masked_score)
            row_top = jnp.max(scores, axis=-1, keepdims=True)
            exponent = jnp.exp(scores - row_top)
            row_total = jnp.sum(exponent, axis=-1, keepdims=True)
            probabilities = (exponent / row_total).astype(jnp.bfloat16)
            context = jnp.einsum(
                "hqk,khd->qhd", probabilities, value_heads, preferred_element_type=jnp.float32
            )
            return (
                context.reshape(block_rows, head_width).astype(jnp.bfloat16),
                (row_top + jnp.log(row_total))[..., 0],
            )

        contexts, block_sums = lax.map(
            one_block, seq_queries.reshape(block_count, block_rows, local_heads, HEAD_DIM)
        )
        return (contexts.reshape(seq_len, head_width), block_sums)

    head_context, log_sums = lax.map(
        attend_forward, (head_layout[0], head_layout[1], head_layout[2], lengths)
    )
    context_rows = lax.all_to_all(
        head_context, "seq", split_axis=1, concat_axis=2, tiled=True
    ).reshape(row_count, model_width)
    attended = matmul_plain(context_rows, full_output) + bias_output
    first_sum = flat_in.astype(jnp.float32) + attended
    first_norm = layer_norm(first_sum, gain_first, shift_first).astype(jnp.bfloat16)
    up_pre = matmul_plain(first_norm, full_up) + bias_up
    hidden_act = gelu_exact(up_pre).astype(jnp.bfloat16)
    down_out = matmul_plain(hidden_act, full_down) + bias_down
    second_sum = first_norm.astype(jnp.float32) + down_out
    layer_out = layer_norm(second_sum, gain_second, shift_second).astype(jnp.bfloat16)
    regathered = (
        lax.all_gather(query_weight, "dp", axis=0, tiled=True),
        lax.all_gather(key_weight, "dp", axis=0, tiled=True),
        lax.all_gather(value_weight, "dp", axis=0, tiled=True),
        lax.all_gather(output_weight, "dp", axis=0, tiled=True),
        lax.all_gather(up_weight, "dp", axis=0, tiled=True),
        lax.all_gather(down_weight, "dp", axis=0, tiled=True),
        lax.all_gather(up_bias, "dp", axis=0, tiled=True),
    )
    full_query, full_key, full_value, full_output, full_up, full_down = regathered[0:6]
    bias_up = regathered[6].astype(jnp.float32)
    positions = lax.axis_index("seq") * local_len + jnp.arange(local_len)
    live_rows = (positions[None, :] < lengths[:, None]).reshape(row_count).astype(jnp.float32)
    grad_out = cotangent.reshape(row_count, model_width).astype(jnp.float32) * live_rows[:, None]
    norm_value, second_pull = jax.vjp(layer_norm, second_sum, gain_second, shift_second)
    second_sum_grad, second_gain_grad, second_shift_grad = second_pull(grad_out)
    down_grad_low = second_sum_grad.astype(jnp.bfloat16)
    down_weight_grad = inner_rows(hidden_act, down_grad_low)
    down_bias_grad = column_sums(down_grad_low)
    grad_hidden = times_transposed(down_grad_low, full_down)
    gelu_value, gelu_pull = jax.vjp(gelu_exact, up_pre)
    (up_grad_full,) = gelu_pull(grad_hidden)
    up_grad_low = up_grad_full.astype(jnp.bfloat16)
    up_weight_grad = inner_rows(first_norm, up_grad_low)
    up_bias_grad = column_sums(up_grad_low)
    first_norm_grad = second_sum_grad + times_transposed(up_grad_low, full_up)
    first_value, first_pull = jax.vjp(layer_norm, first_sum, gain_first, shift_first)
    first_sum_grad, first_gain_grad, first_shift_grad = first_pull(first_norm_grad)
    attended_low = first_sum_grad.astype(jnp.bfloat16)
    output_weight_grad = inner_rows(context_rows, attended_low)
    output_bias_grad = column_sums(attended_low)
    context_grad = times_transposed(attended_low, full_output).astype(jnp.bfloat16)
    grad_heads = lax.all_to_all(
        context_grad.reshape(group_count, local_len, model_width),
        "seq",
        split_axis=2,
        concat_axis=1,
        tiled=True,
    )

    def attend_backward(operands):
        seq_queries, seq_keys, seq_values, seq_grad, seq_sums, length = operands
        key_heads = seq_keys.reshape(seq_len, local_heads, HEAD_DIM)
        value_heads = seq_values.reshape(seq_len, local_heads, HEAD_DIM)
        key_live = jnp.arange(seq_len) < length

        def one_block(running, block_in):
            key_total, value_total = running
            query_block, grad_block, sum_block = block_in
            scores = (
                jnp.einsum(
                    "qhd,khd->hqk", query_block, key_heads, preferred_element_type=jnp.float32
                )
                * score_scale
            )
            scores = jnp.where(key_live[None, None, :], scores, masked_score)
            probabilities = jnp.exp(scores - sum_block[..., None])
            grad_probs = jnp.einsum(
                "qhd,khd->hqk", grad_block, value_heads, preferred_element_type=jnp.float32
            )
            row_delta = jnp.sum(probabilities * grad_probs, axis=-1, keepdims=True)
            grad_scores = (probabilities * (grad_probs - row_delta)).astype(jnp.bfloat16)
            query_grad = (
                jnp.einsum(
                    "hqk,khd->qhd", grad_scores, key_heads, preferred_element_type=jnp.float32
                )
                * score_scale
            )
            key_total = (
                key_total
                + jnp.einsum(
                    "hqk,qhd->khd", grad_scores, query_block, preferred_element_type=jnp.float32
                )
                * score_scale
            )
            value_total = value_total + jnp.einsum(
                "hqk,qhd->khd",
                probabilities.astype(jnp.bfloat16),
                grad_block,
                preferred_element_type=jnp.float32,
            )
            return (
                (key_total, value_total),
                query_grad.reshape(block_rows, head_width).astype(jnp.bfloat16),
            )

        zero_heads = jnp.zeros((seq_len, local_heads, HEAD_DIM), jnp.float32)
        block_shape = (block_count, block_rows, local_heads, HEAD_DIM)
        (key_total, value_total), query_grads = lax.scan(
            one_block,
            (zero_heads, zero_heads),
            (seq_queries.reshape(block_shape), seq_grad.reshape(block_shape), seq_sums),
        )
        return jnp.stack(
            [
                query_grads.reshape(seq_len, head_width),
                key_total.reshape(seq_len, head_width).astype(jnp.bfloat16),
                value_total.reshape(seq_len, head_width).astype(jnp.bfloat16),
            ]
        )

    head_grads = lax.map(
        attend_backward,
        (head_layout[0], head_layout[1], head_layout[2], grad_heads, log_sums, lengths),
    )
    row_grads = lax.all_to_all(head_grads, "seq", split_axis=2, concat_axis=3, tiled=True)
    query_grad_low = row_grads[:, 0].reshape(row_count, model_width)
    key_grad_low = row_grads[:, 1].reshape(row_count, model_width)
    value_grad_low = row_grads[:, 2].reshape(row_count, model_width)
    query_weight_grad = inner_rows(flat_in, query_grad_low)
    key_weight_grad = inner_rows(flat_in, key_grad_low)
    value_weight_grad = inner_rows(flat_in, value_grad_low)
    query_bias_grad = column_sums(query_grad_low)
    value_bias_grad = column_sums(value_grad_low)
    input_grad = (
        first_sum_grad
        + times_transposed(query_grad_low, full_query)
        + times_transposed(key_grad_low, full_key)
        + times_transposed(value_grad_low, full_value)
    ).astype(jnp.bfloat16)
    input_grad = input_grad.reshape(group_count, local_len, model_width)
    summed = (
        lax.psum_scatter(query_weight_grad, "dp", scatter_dimension=0, tiled=True),
        lax.psum_scatter(key_weight_grad, "dp", scatter_dimension=0, tiled=True),
        lax.psum_scatter(value_weight_grad, "dp", scatter_dimension=0, tiled=True),
        lax.psum_scatter(output_weight_grad, "dp", scatter_dimension=0, tiled=True),
        lax.psum_scatter(up_weight_grad, "dp", scatter_dimension=0, tiled=True),
        lax.psum_scatter(down_weight_grad, "dp", scatter_dimension=0, tiled=True),
        lax.psum_scatter(query_bias_grad, "dp", scatter_dimension=0, tiled=True),
        lax.psum_scatter(value_bias_grad, "dp", scatter_dimension=0, tiled=True),
        lax.psum_scatter(output_bias_grad, "dp", scatter_dimension=0, tiled=True),
        lax.psum_scatter(up_bias_grad, "dp", scatter_dimension=0, tiled=True),
        lax.psum_scatter(down_bias_grad, "dp", scatter_dimension=0, tiled=True),
        lax.psum_scatter(first_gain_grad, "dp", scatter_dimension=0, tiled=True),
        lax.psum_scatter(first_shift_grad, "dp", scatter_dimension=0, tiled=True),
        lax.psum_scatter(second_gain_grad, "dp", scatter_dimension=0, tiled=True),
        lax.psum_scatter(second_shift_grad, "dp", scatter_dimension=0, tiled=True),
    )
    totals = lax.psum(
        (
            summed[0],
            summed[1],
            summed[2],
            summed[3],
            summed[4],
            summed[5],
            summed[6],
            summed[7],
            summed[8],
            summed[9],
            summed[10],
            summed[11],
            summed[12],
            summed[13],
            summed[14],
        ),
        "seq",
    )
    layer_out = layer_out.reshape(group_count, local_len, model_width)
    return (
        layer_out,
        input_grad,
        totals[0],
        totals[1],
        totals[2],
        totals[3],
        totals[4],
        totals[5],
        totals[6],
        totals[7],
        totals[8],
        totals[9],
        totals[10],
        totals[11],
        totals[12],
        totals[13],
        totals[14],
    )


def solution(mesh):
    return jax.shard_map(
        local,
        mesh=mesh,
        in_specs=(
            P("dp", "seq", None),
            P("dp"),
            P("dp", None),
            P("dp", None),
            P("dp", None),
            P("dp", None),
            P("dp", None),
            P("dp", None),
            P("dp"),
            P("dp"),
            P("dp"),
            P("dp"),
            P("dp"),
            P("dp"),
            P("dp"),
            P("dp"),
            P("dp"),
            P("dp", "seq", None),
        ),
        out_specs=(
            P("dp", "seq", None),
            P("dp", "seq", None),
            P("dp", None),
            P("dp", None),
            P("dp", None),
            P("dp", None),
            P("dp", None),
            P("dp", None),
            P("dp"),
            P("dp"),
            P("dp"),
            P("dp"),
            P("dp"),
            P("dp"),
            P("dp"),
            P("dp"),
            P("dp"),
        ),
        check_vma=False,
    )
```

profile of v0, /device:TPU:0, one launch (start us, length us, event | category | flops | bytes accessed | tf_op | source)
XLA Modules:
  0.0 1238.4 jit_solution(14016261787662703552)
XLA Ops:
  19.3 39.9 %all-reduce.20 = (bf16[768]{0:T(1024)(128)(2,1)S(1)}, bf16[768]{0:T(1024)(128)(2,1)S(1)}, bf16[768]{0:T(1024)(128)(2,1)}, bf16[768]{0:T(1024)(128)(2,1)}, bf16[7...) all-reduce(bf16[768]{0:T(1024)(128)(2,1)S(1)} %dynamic-update-slice, ...), channel_id=1, replica_groups=mesh['dp'=8,'seq'=4] {'dp'}, use_global_device_ids=true, to_apply=%add.1 | all-reduce | flops 6144 | bytes 24576
  62.1 34.2 %all-gather.12.cloned.1.call-done = bf16[768,768]{1,0:T(8,128)(2,1)} async-done(((bf16[96,768]{1,0:T(8,128)(2,1)}), bf16[768,768]{1,0:T(8,128)(2,1)}) %all-gather.12.cloned.1.call-update) | async-done | bytes 1179664 | tf_op jit(solution)/shard_map/all_gather | solution.py:65
  99.0 39.3 %all-gather.10.cloned.1.call-done = bf16[768,768]{1,0:T(8,128)(2,1)} async-done(((bf16[96,768]{1,0:T(8,128)(2,1)}), bf16[768,768]{1,0:T(8,128)(2,1)}) %all-gather.10.cloned.1.call-update) | async-done | bytes 1179664 | tf_op jit(solution)/shard_map/all_gather | solution.py:64
  141.1 4.3 pad_maximum_fusion
  149.7 27.9 %all-to-all-done = bf16[3,2,256,768]{2,1,0,3:T(2,128)(2,1)S(1)} async-done(((bf16[3,2,256,768]{2,1,0,3:T(2,128)(2,1)}), bf16[3,2,256,768]{2,1,0,3:T(2,128)(2,1)S(1)}, u32[]{:S(2)}, u32[]{:S(2)}) %all-to-all-start) | async-done | bytes 2359328 | tf_op jit(solution)/shard_map/all_to_all | solution.py:98
  183.4 29.9 %while.51 = (s32[]{:T(128)}, bf16[2,1024,192]{2,1,0:T(8,128)(2,1)}, f32[2,2,3,512]{3,2,1,0:T(4,128)S(1)}, bf16[2,1024,192]{1,2,0:T(8,128)(2,1)}, bf16[2,1024,192...) while((s32[]{:T(128)}, bf16[2,1024,192]{2,1,0:T(8,128)(2,1)}, ...), condition=%wide.region_5.6_spmd, body=%wide.region_0.5_spmd.sunk | while | flops 421625344 | bytes 26176296 | solution.py:137
  186.4 10.9 while.54
  201.4 10.9 while.54
  220.4 26.8 %all-gather = bf16[8,1,384]{2,1,0:T(2,128)(2,1)S(1)} all-gather(bf16[1,1,384]{2,1,0:T(2,128)(2,1)S(1)} %reshape.301), channel_id=1, replica_groups=mesh['dp'=8,'seq'=4] {'dp'}, dimensions={0}, use_global_device_ids=true | all-gather | bytes 6912 | tf_op jit(solution)/shard_map/all_gather | solution.py:72
  253.7 7.6 all-gather.16.cloned.1.call-done
  261.3 20.9 %multiply_convert_fusion.1 = (bf16[512,3072]{1,0:T(8,128)(2,1)}, f32[512,3072]{1,0:T(8,128)}, f32[512,3072]{1,0:T(8,128)}) fusion(f32[3072]{0:T(1024)S(1)} %bitcast.268, bf16[768,3072]{1,0:T(8,128)(2,1)} %all-gather.16.cloned.1.call-done, f32[512,768]{1,0:T(8,128)} %copy-done.21, f32[768]{0:T(1024)S(1)} %convert_element_type.180, ...), kind=kOutput, calls=%fused_computation.66 | convolution fusion | flops 2521694208 | bytes 22042624 | tf_op jit(solution)/shard_map/dot_general | solution.py:23
  282.2 59.2 %all-gather.18.cloned.1.call-done = bf16[3072,768]{1,0:T(8,128)(2,1)} async-done(((bf16[384,768]{1,0:T(8,128)(2,1)}), bf16[3072,768]{1,0:T(8,128)(2,1)}) %all-gather.18.cloned.1.call-update) | async-done | bytes 4718608 | tf_op jit(solution)/shard_map/all_gather | solution.py:68
  341.4 6.1 fusion.61
  351.7 9.0 convert_reduce_fusion
  374.1 11.6 all-to-all-done.2
  385.9 70.7 %while.53 = (s32[]{:T(128)}, bf16[2,3,1024,192]{2,3,1,0:T(8,128)(2,1)}, bf16[2,1024,192]{1,2,0:T(8,128)(2,1)}, bf16[2,1024,192]{1,2,0:T(8,128)(2,1)S(1)}, f32[2,...) while((s32[]{:T(128)}, ...), condition=%wide.region_18.19_spmd, body=%wide.region_14.18_spmd.sunk | while | flops 1035337216 | bytes 144484816 | solution.py:252
  389.2 27.8 %while.55 = (s32[]{:T(128)}, f32[1024,3,64]{0,2,1:T(8,128)}, f32[1024,3,64]{0,2,1:T(8,128)}, bf16[2,512,192]{1,2,0:T(8,128)(2,1)}, bf16[2,512,3,64]{1,3,2,0:T(8,...) while((s32[]{:T(128)}, f32[1024,3,64]{0,2,1:T(8,128)}, ...), condition=%wide.region_17.17_spmd.clone, body=%wide.region_15.16_spmd.clone.sunk | while | flops 1031405056 | bytes 115951104 | solution.py:239
  424.4 27.8 %while.55 = (s32[]{:T(128)}, f32[1024,3,64]{0,2,1:T(8,128)}, f32[1024,3,64]{0,2,1:T(8,128)}, bf16[2,512,192]{1,2,0:T(8,128)(2,1)}, bf16[2,512,3,64]{1,3,2,0:T(8,...) while((s32[]{:T(128)}, f32[1024,3,64]{0,2,1:T(8,128)}, ...), condition=%wide.region_17.17_spmd.clone, body=%wide.region_15.16_spmd.clone.sunk | while | flops 1031405056 | bytes 115951104 | solution.py:239
  456.6 7.5 copy.120
  464.1 40.3 %all_to_all.66 = bf16[2,3,1024,192]{3,0,1,2:T(2,128)(2,1)} all-to-all(bf16[2,3,1024,192]{3,0,1,2:T(2,128)(2,1)S(1)} %copy.120), channel_id=1, replica_groups=mesh['dp'=8,'seq'=4] {'seq'}, dimensions={2} | all-to-all | bytes 4718592 | tf_op jit(solution)/shard_map/all_to_all | solution.py:256
  504.3 9.0 copy.129
  546.5 8.9 fusion.62
  555.5 8.5 fusion.66
  564.0 28.1 %reduce-scatter.19.cloned.1.call-done = f32[96,768]{1,0:T(8,128)} async-done(((f32[768,768]{1,0:T(8,128)}), f32[96,768]{1,0:T(8,128)}) %reduce-scatter.19.cloned.1.call-update) | async-done | bytes 294928
  594.0 69.7 %reduce-scatter.21.cloned.1.call-done = f32[96,768]{1,0:T(8,128)} async-done(((f32[768,768]{1,0:T(8,128)}), f32[96,768]{1,0:T(8,128)}) %reduce-scatter.21.cloned.1.call-update) | async-done | bytes 294928
  665.6 69.7 %reduce-scatter.23.cloned.1.call-done = f32[96,768]{1,0:T(8,128)} async-done(((f32[768,768]{1,0:T(8,128)}), f32[96,768]{1,0:T(8,128)}) %reduce-scatter.23.cloned.1.call-update) | async-done | bytes 294928
  737.2 69.5 %reduce-scatter.13.cloned.1.call-done = f32[96,768]{1,0:T(8,128)} async-done(((f32[768,768]{1,0:T(8,128)}), f32[96,768]{1,0:T(8,128)}) %reduce-scatter.13.cloned.1.call-update) | async-done | bytes 294928 | tf_op jit(solution)/shard_map/reduce_scatter | solution.py:276
  806.8 166.1 %reduce-scatter.15.cloned.1.call-done = f32[96,3072]{1,0:T(8,128)} async-done(((f32[768,3072]{1,0:T(8,128)}), f32[96,3072]{1,0:T(8,128)}) %reduce-scatter.15.cloned.1.call-update) | async-done | bytes 1179664 | tf_op jit(solution)/shard_map/reduce_scatter | solution.py:277
  972.9 166.0 %reduce-scatter.17.cloned.1.call-done = f32[384,768]{1,0:T(8,128)} async-done(((f32[3072,768]{1,0:T(8,128)}), f32[384,768]{1,0:T(8,128)}) %reduce-scatter.17.cloned.1.call-update) | async-done | bytes 1179664 | tf_op jit(solution)/shard_map/reduce_scatter | solution.py:278
  1142.0 35.7 %all-reduce.17 = (f32[768]{0:T(1024)S(1)}, f32[768]{0:T(1024)S(1)}, f32[768]{0:T(1024)S(1)}, f32[3072]{0:T(1024)S(1)}, f32[768]{0:T(1024)S(1)}, /*index=5*/f32[7...) all-reduce(f32[768]{0:T(1024)S(1)} %get-tuple-element.403, ...), channel_id=8, replica_groups=mesh['dp'=8,'seq'=4] {'dp'}, use_global_device_ids=true, to_apply=%region_32.33.clone | all-reduce | flops 9216 | bytes 73728
  1178.4 6.3 all-reduce.18
  1191.2 31.0 %all-reduce.23.cloned.1.call-done = (f32[96,768]{0,1:T(8,128)}, f32[96,768]{0,1:T(8,128)}, f32[96,768]{0,1:T(8,128)}, f32[96,768]{1,0:T(8,128)}, f32[96,3072]{1,0:T(8,128)}, /*index=5*/f32[384,768]{1,0:T(8,128)}) async-done(((f32[96,768]{0,1:T(8,128)}, f32[96,768]{0,1:T(8,128)}, f32[96,768]{0,1:T(8,128)}, f32[96,768]{1,0:T(8,128)}, f32[96,3072]{1,0:T(8,128)}, /*index=5*/f32[384,768]{1,0:T(8,128)}), ...) | async-done | bytes 3538960 | tf_op jit(solution)/shard_map/psum | solution.py:289
  (465 shorter events, 217.0 us)
Async XLA Ops:
  7.2 52.0 %all-gather.8.cloned.1.call-start = ((), (), s32[]{:S(2)}) async-start(), calls=%async_computation.10 | async-start | bytes 1327104 | tf_op jit(solution)/shard_map/all_gather | solution.py:63
  7.9 88.4 %all-gather.12.cloned.1.call-start = ((), (), s32[]{:S(2)}) async-start(), calls=%async_computation.12 | async-start | bytes 1327104 | tf_op jit(solution)/shard_map/all_gather | solution.py:65
  8.7 129.7 %all-gather.10.cloned.1.call-start = ((), (), s32[]{:S(2)}) async-start(), calls=%async_computation.11 | async-start | bytes 1327104 | tf_op jit(solution)/shard_map/all_gather | solution.py:64
  9.4 240.4 %all-gather.14.cloned.1.call-start = ((), (), s32[]{:S(2)}) async-start(), calls=%async_computation.13 | async-start | bytes 1327104 | tf_op jit(solution)/shard_map/all_gather | solution.py:66
  10.0 251.3 %all-gather.16.cloned.1.call-start = ((), (), s32[]{:S(2)}) async-start(), calls=%async_computation.14 | async-start | bytes 5308416 | tf_op jit(solution)/shard_map/all_gather | solution.py:67
  10.6 85.7 %copy-start.18 = (bf16[2,256,768]{2,1,0:T(8,128)(2,1)S(1)}, bf16[2,256,768]{2,1,0:T(8,128)(2,1)}, u32[]{:S(2)}) copy-start(bf16[2,256,768]{2,1,0:T(8,128)(2,1)} %param.26) | copy-start | bytes 2359300
  145.4 32.1 %all-to-all-start = ((bf16[3,2,256,768]{2,1,0,3:T(2,128)(2,1)}), bf16[3,2,256,768]{2,1,0,3:T(2,128)(2,1)S(1)}, u32[]{:S(2)}, u32[]{:S(2)}) async-start(bf16[3,2,256,768]{2,1,0,3:T(2,128)(2,1)} %pad_maximum_fusion), calls=%async_computation | async-start | bytes 4718592 | tf_op jit(solution)/shard_map/all_to_all | solution.py:98
  149.1 192.3 %all-gather.18.cloned.1.call-start = ((), (), s32[]{:S(2)}) async-start(), calls=%async_computation.15 | async-start | bytes 5308416 | tf_op jit(solution)/shard_map/all_gather | solution.py:68
  213.3 33.9 %copy-start.52 = (bf16[768]{0:T(1024)(128)(2,1)S(1)}, bf16[768]{0:T(1024)(128)(2,1)}, u32[]{:S(2)}) copy-start(bf16[768]{0:T(1024)(128)(2,1)} %get-tuple-element.500) | copy-start | bytes 4612
  213.3 34.6 %copy-start.51 = (bf16[768]{0:T(1024)(128)(2,1)S(1)}, bf16[768]{0:T(1024)(128)(2,1)}, u32[]{:S(2)}) copy-start(bf16[768]{0:T(1024)(128)(2,1)} %get-tuple-element.499) | copy-start | bytes 4612
  216.7 31.3 %all-to-all-start.1 = ((bf16[2,1024,192]{2,0,1:T(2,128)(2,1)}), bf16[2,1024,192]{2,0,1:T(2,128)(2,1)S(1)}, u32[]{:S(2)}, u32[]{:S(2)}) async-start(bf16[2,1024,192]{2,0,1:T(2,128)(2,1)} %copy.115), calls=%async_computation.1 | async-start | bytes 2097152 | tf_op jit(solution)/shard_map/all_to_all | solution.py:140
  220.4 144.1 %copy-start.41 = (f32[768]{0:T(1024)}, f32[768]{0:T(1024)S(1)}, u32[]{:S(2)}) copy-start(f32[768]{0:T(1024)S(1)} %convert_element_type.179) | copy-start | bytes 9220
  220.4 121.0 %copy-start.47 = (f32[768]{0:T(1024)}, f32[768]{0:T(1024)S(1)}, u32[]{:S(2)}) copy-start(f32[768]{0:T(1024)S(1)} %convert_element_type.180) | copy-start | bytes 9220
  252.3 112.2 %copy-start.34 = (f32[512]{0:T(512)}, f32[512]{0:T(512)S(1)}, u32[]{:S(2)}) copy-start(f32[512]{0:T(512)S(1)} %broadcast_multiply_fusion.1) | copy-start | bytes 6148
  253.7 110.7 %copy-start.44 = (f32[512]{0:T(512)}, f32[512]{0:T(512)S(1)}, u32[]{:S(2)}) copy-start(f32[512]{0:T(512)S(1)} %fusion.51) | copy-start | bytes 6148
  261.3 80.1 %copy-start.22 = (f32[512,768]{1,0:T(8,128)S(1)}, f32[512,768]{1,0:T(8,128)}, u32[]{:S(2)}) copy-start(f32[512,768]{1,0:T(8,128)} %copy-done.21) | copy-start | bytes 4718596
  370.5 15.1 %all-to-all-start.2 = ((bf16[2,256,768]{1,0,2:T(2,128)(2,1)}), bf16[2,256,768]{1,0,2:T(2,128)(2,1)S(1)}, u32[]{:S(2)}, u32[]{:S(2)}) async-start(bf16[2,256,768]{1,0,2:T(2,128)(2,1)} %copy.117), calls=%async_computation.2 | async-start | bytes 1572864 | tf_op jit(solution)/shard_map/all_to_all | solution.py:183
  374.0 218.1 %reduce-scatter.19.cloned.1.call-start = ((), (), s32[]{:S(2)}) async-start(), calls=%async_computation.19 | async-start | bytes 2654208
  525.7 138.0 %reduce-scatter.21.cloned.1.call-start = ((), (), s32[]{:S(2)}) async-start(), calls=%async_computation.20 | async-start | bytes 2654208
  534.4 200.9 %reduce-scatter.23.cloned.1.call-start = ((), (), s32[]{:S(2)}) async-start(), calls=%async_computation.21 | async-start | bytes 2654208
  542.7 264.1 %reduce-scatter.13.cloned.1.call-start = ((), (), s32[]{:S(2)}) async-start(), calls=%async_computation.16 | async-start | bytes 2654208 | tf_op jit(solution)/shard_map/reduce_scatter | solution.py:276
  546.4 426.5 %reduce-scatter.15.cloned.1.call-start = ((), (), s32[]{:S(2)}) async-start(), calls=%async_computation.17 | async-start | bytes 10616832 | tf_op jit(solution)/shard_map/reduce_scatter | solution.py:277
  555.4 583.5 %reduce-scatter.17.cloned.1.call-start = ((), (), s32[]{:S(2)}) async-start(), calls=%async_computation.18 | async-start | bytes 10616832 | tf_op jit(solution)/shard_map/reduce_scatter | solution.py:278
  563.9 576.3 %copy-start.46 = (f32[2,256]{1,0:T(2,128)S(1)}, f32[2,256]{1,0:T(2,128)}, u32[]{:S(2)}) copy-start(f32[2,256]{1,0:T(2,128)} %get-tuple-element.530) | copy-start | bytes 6148
  564.0 658.2 %all-reduce.23.cloned.1.call-start = ((), (), s32[]{:S(2)}) async-start(), calls=%async_computation.22 | async-start | bytes 7667712 | tf_op jit(solution)/shard_map/psum | solution.py:289
  737.2 404.7 %copy-start.38 = (f32[768]{0:T(1024)S(1)}, f32[768]{0:T(1024)}, u32[]{:S(2)}) copy-start(f32[768]{0:T(1024)} %get-tuple-element.400) | copy-start | bytes 9220
  737.2 404.7 %copy-start.39 = (f32[768]{0:T(1024)S(1)}, f32[768]{0:T(1024)}, u32[]{:S(2)}) copy-start(f32[768]{0:T(1024)} %get-tuple-element.501) | copy-start | bytes 9220
  737.2 404.7 %copy-start.40 = (f32[768]{0:T(1024)S(1)}, f32[768]{0:T(1024)}, u32[]{:S(2)}) copy-start(f32[768]{0:T(1024)} %get-tuple-element.505) | copy-start | bytes 9220
  737.2 404.7 %copy-start.43 = (f32[3072]{0:T(1024)S(1)}, f32[3072]{0:T(1024)}, u32[]{:S(2)}) copy-start(f32[3072]{0:T(1024)} %get-tuple-element.503) | copy-start | bytes 36868
  737.2 404.7 %copy-start.49 = (f32[768]{0:T(1024)S(1)}, f32[768]{0:T(1024)}, u32[]{:S(2)}) copy-start(f32[768]{0:T(1024)} %get-tuple-element.398) | copy-start | bytes 9220
  737.2 404.7 %copy-start.50 = (f32[768]{0:T(1024)S(1)}, f32[768]{0:T(1024)}, u32[]{:S(2)}) copy-start(f32[768]{0:T(1024)} %get-tuple-element.404) | copy-start | bytes 9220
  1141.9 45.3 %copy-start.23 = (bf16[2,1,256,768]{3,2,0,1:T(8,128)(2,1)S(1)}, bf16[2,1,256,768]{3,2,0,1:T(8,128)(2,1)}, u32[]{:S(2)}) copy-start(bf16[2,1,256,768]{3,2,0,1:T(8,128)(2,1)} %copy.124) | copy-start | bytes 2359300
  (91 other events, 367.7 us)
Sparse Core Ops, SparseCore 0:
  10.2 43.9 all-gather.7
  56.4 39.8 all-gather.11
  98.5 39.8 all-gather.9
  140.4 39.8 all-gather.13
  182.4 78.8 all-gather.15
  263.3 78.0 all-gather.17
  525.8 66.2 reduce-scatter.18
  595.6 68.0 reduce-scatter.20
  667.2 68.0 reduce-scatter.22
  738.7 68.0 reduce-scatter.12
  810.4 162.4 reduce-scatter.14
  976.3 162.5 reduce-scatter.16
  1142.3 79.8 all-reduce.22
where the time goes:
time: 1250 us; the launch traced here: 1240 us
  waiting for transfers between devices  784 us (63%)
  blocking collectives  149 us (12%)
  matrix products  141 us (11%)
  local copies, waits for them, and re-layouts  98.8 us (8%)
  other arithmetic  36 us (3%)
  between operations  16.9 us (1%)
    unnamed x16, waiting for transfers between devices  171 us
    reduce_scatter x1, waiting for transfers between devices, local(): lax.psum_scatter(up_weight_grad, 'dp', scatter_dimension=0, tiled=True)  166 us
    reduce_scatter x1, waiting for transfers between devices, local(): lax.psum_scatter(down_weight_grad, 'dp', scatter_dimension=0, tiled=True)  166 us
    unnamed x2, blocking collectives  75.6 us
    reduce_scatter x1, waiting for transfers between devices, local(): lax.psum_scatter(output_weight_grad, 'dp', scatter_dimension=0, tiled=True)  69.5 us
    all_gather x1, waiting for transfers between devices, local(): lax.all_gather(down_weight, 'dp', axis=0, tiled=True)  59.2 us
    all_to_all x1, blocking collectives, local(): lax.all_to_all(head_grads, 'seq', split_axis=2, concat_axis=3, tiled=True)  40.3 us
    all_gather x1, waiting for transfers between devices, local(): lax.all_gather(key_weight, 'dp', axis=0, tiled=True)  39.3 us
  transfers between devices with their start and end apart: 16, of which 13 were waited for; matrix products, arithmetic and copies ran while one was open for 11% of the time, Pallas kernels for 0%

commit v1 on v0

--- a/solution.py
+++ b/solution.py
@@ -6,6 +6,28 @@
 HEAD_DIM = 64
 eps_norm = 1e-05
 masked_score = -1000000000.0
+
+
+def laid_out(blocks, dim):
+    blocks = jnp.moveaxis(blocks, 0, dim)
+    dims = blocks.shape
+    return blocks.reshape(*dims[:dim], dims[dim] * dims[dim + 1], *dims[dim + 2 :])
+
+
+def ring_gather(shard, axis, dim):
+    size = lax.axis_size(axis)
+    pairs = [(i, (i + 1) % size) for i in range(size)]
+    back = [(b, a) for a, b in pairs]
+    lower, upper = ([], [])
+    for lap in range(size - 1):
+        if lap % 2 == 0:
+            lower.append(lax.ppermute(lower[-1] if lower else shard, axis, pairs))
+        else:
+            upper.append(lax.ppermute(upper[-1] if upper else shard, axis, back))
+    blocks = jnp.stack([*lower[::-1], shard, *upper])
+    shift = lax.axis_index(axis) - len(lower)
+    blocks = blocks[(jnp.arange(size) - shift) % size]
+    return laid_out(blocks, dim)
 
 
 def layer_norm(hidden, gain_vec, shift_vec):
@@ -62,7 +84,7 @@
     gathered = (
         lax.all_gather(query_weight, "dp", axis=0, tiled=True),
         lax.all_gather(key_weight, "dp", axis=0, tiled=True),
-        lax.all_gather(value_weight, "dp", axis=0, tiled=True),
+        ring_gather(value_weight, "dp", 0),
         lax.all_gather(output_weight, "dp", axis=0, tiled=True),
         lax.all_gather(up_weight, "dp", axis=0, tiled=True),
         lax.all_gather(down_weight, "dp", axis=0, tiled=True),

time: 1250 us -> 1250 us (level)
  waiting for transfers between devices: 784 us -> 762 us
  starting transfers between devices: 11.7 us -> 26.1 us
  local copies, waits for them, and re-layouts: 98.8 us -> 113 us
    all_gather x1, waiting for transfers between devices: 39.3 us -> 0.05 us  [local(): lax.all_gather(key_weight, 'dp', axis=0, tiled=True)]
    psum x1, waiting for transfers between devices: 31 us -> 68.1 us  [local(): lax.psum((summed[0], summed[1], summed[2], summed[3], summed[4], summed[5...]
    all_gather x1, waiting for transfers between devices: 34.2 us -> 0.01 us  [local(): lax.all_gather(value_weight, 'dp', axis=0, tiled=True)]
    ppermute x0 -> x7, waiting for transfers between devices: none -> 24.4 us  [the longest x4 16.3 us: ring_gather(): lower.append(lax.ppermute(lower[-1] if lower else shard, axis, pairs))]
    ppermute x0 -> x7, starting transfers between devices: none -> 13.7 us  [the longest x3 9.23 us: ring_gather(): upper.append(lax.ppermute(upper[-1] if upper else shard, axis, back))]
    unnamed x131 -> x136, local copies, waits for them, and re-layouts: 36.7 us -> 38.6 us
  transfers between devices with their start and end apart: 16 -> 23, of which waited for: 13 -> 14; matrix products, arithmetic and copies ran while one was open for 11% -> 12% of each run, Pallas kernels for 0% -> 0%
where the time goes in v1:
time: 1250 us
  waiting for transfers between devices  762 us (61%)
  blocking collectives  146 us (12%)
  matrix products  146 us (12%)
  local copies, waits for them, and re-layouts  113 us (9%)
  other arithmetic  36.4 us (3%)
  starting transfers between devices  26.1 us (2%)
  between operations  16.9 us (1%)
    unnamed x16, waiting for transfers between devices  170 us
    reduce_scatter x1, waiting for transfers between devices, local(): lax.psum_scatter(up_weight_grad, 'dp', scatter_dimension=0, tiled=True)  166 us
    reduce_scatter x1, waiting for transfers between devices, local(): lax.psum_scatter(down_weight_grad, 'dp', scatter_dimension=0, tiled=True)  166 us
    unnamed x2, blocking collectives  73.1 us
    reduce_scatter x1, waiting for transfers between devices, local(): lax.psum_scatter(output_weight_grad, 'dp', scatter_dimension=0, tiled=True)  69.9 us
    psum x1, waiting for transfers between devices, local(): lax.psum((summed[0], summed[1], summed[2], summed[3], summed[4], summed[5...  68.1 us
    all_gather x1, waiting for transfers between devices, local(): lax.all_gather(down_weight, 'dp', axis=0, tiled=True)  57.1 us
    all_to_all x1, blocking collectives, local(): lax.all_to_all(head_grads, 'seq', split_axis=2, concat_axis=3, tiled=True)  40.3 us
  transfers between devices with their start and end apart: 23, of which 14 were waited for; matrix products, arithmetic and copies ran while one was open for 12% of the time, Pallas kernels for 0%

profile of v1, /device:TPU:0, one launch (start us, length us, event | category | flops | bytes accessed | tf_op | source)
XLA Modules:
  0.0 1247.1 jit_solution(6676058342330993932)
XLA Ops:
  13.0 7.1 collective-permute-done
  24.8 5.9 collective-permute-done.1
  48.7 37.1 %all-reduce.20 = (bf16[768]{0:T(1024)(128)(2,1)S(1)}, bf16[768]{0:T(1024)(128)(2,1)S(1)}, bf16[768]{0:T(1024)(128)(2,1)}, bf16[768]{0:T(1024)(128)(2,1)}, bf16[7...) all-reduce(bf16[768]{0:T(1024)(128)(2,1)S(1)} %dynamic-update-slice, ...), channel_id=1, replica_groups=mesh['dp'=8,'seq'=4] {'dp'}, use_global_device_ids=true, to_apply=%add.1 | all-reduce | flops 6144 | bytes 24576
  86.0 8.1 collective-permute-done.6
  112.9 27.9 %all-to-all-done = bf16[3,2,256,768]{2,1,0,3:T(2,128)(2,1)S(1)} async-done(((bf16[3,2,256,768]{2,1,0,3:T(2,128)(2,1)}), bf16[3,2,256,768]{2,1,0,3:T(2,128)(2,1)S(1)}, u32[]{:S(2)}, u32[]{:S(2)}) %all-to-all-start) | async-done | bytes 2359328 | tf_op jit(solution)/shard_map/all_to_all | solution.py:120
  147.0 33.4 %while.51 = (s32[]{:T(128)}, bf16[2,1024,192]{2,1,0:T(8,128)(2,1)}, f32[2,2,3,512]{3,2,1,0:T(4,128)}, bf16[2,1024,192]{1,2,0:T(8,128)(2,1)S(1)}, bf16[2,1024,192...) while((s32[]{:T(128)}, bf16[2,1024,192]{2,1,0:T(8,128)(2,1)}, ...), condition=%wide.region_5.6_spmd, body=%wide.region_0.5_spmd.sunk | while | flops 421625344 | bytes 27946360 | solution.py:159
  148.8 12.3 while.54
  165.4 12.3 while.54
  188.4 26.4 %all-gather = bf16[8,1,384]{2,1,0:T(2,128)(2,1)S(1)} all-gather(bf16[1,1,384]{2,1,0:T(2,128)(2,1)S(1)} %reshape.362), channel_id=1, replica_groups=mesh['dp'=8,'seq'=4] {'dp'}, dimensions={0}, use_global_device_ids=true | all-gather | bytes 6912 | tf_op jit(solution)/shard_map/all_gather | solution.py:94
  215.6 6.1 copy.116
  227.8 20.8 %multiply_convert_fusion.1 = (bf16[512,3072]{1,0:T(8,128)(2,1)}, f32[512,3072]{1,0:T(8,128)}, f32[512,3072]{1,0:T(8,128)}) fusion(f32[3072]{0:T(1024)S(1)} %bitcast.289, bf16[768,3072]{1,0:T(8,128)(2,1)} %all-gather.14.cloned.1.call-done, f32[512,768]{1,0:T(8,128)} %copy-done.24, f32[768]{0:T(1024)S(1)} %convert_element_type.184, ...), kind=kOutput, calls=%fused_computation.67 | convolution fusion | flops 2521694208 | bytes 22042624 | tf_op jit(solution)/shard_map/dot_general | solution.py:45
  248.6 57.1 %all-gather.16.cloned.1.call-done = bf16[3072,768]{1,0:T(8,128)(2,1)} async-done(((bf16[384,768]{1,0:T(8,128)(2,1)}), bf16[3072,768]{1,0:T(8,128)(2,1)}) %all-gather.16.cloned.1.call-update) | async-done | bytes 4718608 | tf_op jit(solution)/shard_map/all_gather | solution.py:90
  305.7 6.5 fusion.63
  316.5 9.0 convert_reduce_fusion
  338.2 11.6 all-to-all-done.2
  350.9 71.7 %while.53 = (s32[]{:T(128)}, bf16[2,3,1024,192]{2,3,1,0:T(8,128)(2,1)}, bf16[2,1024,192]{1,2,0:T(8,128)(2,1)S(1)}, bf16[2,1024,192]{1,2,0:T(8,128)(2,1)}, f32[2,...) while((s32[]{:T(128)}, ...), condition=%wide.region_18.19_spmd, body=%wide.region_14.18_spmd.sunk | while | flops 1035337216 | bytes 150579664 | solution.py:274
  354.5 27.9 %while.55 = (s32[]{:T(128)}, f32[1024,3,64]{0,2,1:T(8,128)}, f32[1024,3,64]{0,2,1:T(8,128)}, bf16[2,512,192]{1,2,0:T(8,128)(2,1)}, bf16[2,512,3,64]{1,3,2,0:T(8,...) while((s32[]{:T(128)}, f32[1024,3,64]{0,2,1:T(8,128)}, ...), condition=%wide.region_17.17_spmd.clone, body=%wide.region_15.16_spmd.clone.sunk | while | flops 1031405056 | bytes 115951104 | solution.py:261
  390.3 27.9 %while.55 = (s32[]{:T(128)}, f32[1024,3,64]{0,2,1:T(8,128)}, f32[1024,3,64]{0,2,1:T(8,128)}, bf16[2,512,192]{1,2,0:T(8,128)(2,1)}, bf16[2,512,3,64]{1,3,2,0:T(8,...) while((s32[]{:T(128)}, f32[1024,3,64]{0,2,1:T(8,128)}, ...), condition=%wide.region_17.17_spmd.clone, body=%wide.region_15.16_spmd.clone.sunk | while | flops 1031405056 | bytes 115951104 | solution.py:261
  422.6 7.5 copy.120
  430.1 40.3 %all_to_all.66 = bf16[2,3,1024,192]{3,0,1,2:T(2,128)(2,1)} all-to-all(bf16[2,3,1024,192]{3,0,1,2:T(2,128)(2,1)S(1)} %copy.120), channel_id=1, replica_groups=mesh['dp'=8,'seq'=4] {'seq'}, dimensions={2} | all-to-all | bytes 4718592 | tf_op jit(solution)/shard_map/all_to_all | solution.py:278
  470.4 9.1 copy.129
  512.5 8.4 fusion.68
  521.6 9.0 fusion.64
  531.2 27.1 %reduce-scatter.19.cloned.1.call-done = f32[96,768]{1,0:T(8,128)} async-done(((f32[768,768]{1,0:T(8,128)}), f32[96,768]{1,0:T(8,128)}) %reduce-scatter.19.cloned.1.call-update) | async-done | bytes 294928
  560.2 69.8 %reduce-scatter.21.cloned.1.call-done = f32[96,768]{1,0:T(8,128)} async-done(((f32[768,768]{1,0:T(8,128)}), f32[96,768]{1,0:T(8,128)}) %reduce-scatter.21.cloned.1.call-update) | async-done | bytes 294928
  631.9 69.9 %reduce-scatter.23.cloned.1.call-done = f32[96,768]{1,0:T(8,128)} async-done(((f32[768,768]{1,0:T(8,128)}), f32[96,768]{1,0:T(8,128)}) %reduce-scatter.23.cloned.1.call-update) | async-done | bytes 294928
  703.6 69.9 %reduce-scatter.13.cloned.1.call-done = f32[96,768]{1,0:T(8,128)} async-done(((f32[768,768]{1,0:T(8,128)}), f32[96,768]{1,0:T(8,128)}) %reduce-scatter.13.cloned.1.call-update) | async-done | bytes 294928 | tf_op jit(solution)/shard_map/reduce_scatter | solution.py:298
  773.5 166.0 %reduce-scatter.17.cloned.1.call-done = f32[384,768]{1,0:T(8,128)} async-done(((f32[3072,768]{1,0:T(8,128)}), f32[384,768]{1,0:T(8,128)}) %reduce-scatter.17.cloned.1.call-update) | async-done | bytes 1179664 | tf_op jit(solution)/shard_map/reduce_scatter | solution.py:300
  939.5 166.2 %reduce-scatter.15.cloned.1.call-done = f32[96,3072]{1,0:T(8,128)} async-done(((f32[768,3072]{1,0:T(8,128)}), f32[96,3072]{1,0:T(8,128)}) %reduce-scatter.15.cloned.1.call-update) | async-done | bytes 1179664 | tf_op jit(solution)/shard_map/reduce_scatter | solution.py:299
  1108.8 36.1 %all-reduce.17 = (f32[768]{0:T(1024)S(1)}, f32[768]{0:T(1024)S(1)}, f32[768]{0:T(1024)S(1)}, f32[3072]{0:T(1024)S(1)}, f32[768]{0:T(1024)S(1)}, /*index=5*/f32[7...) all-reduce(f32[768]{0:T(1024)S(1)} %get-tuple-element.403, ...), channel_id=8, replica_groups=mesh['dp'=8,'seq'=4] {'dp'}, use_global_device_ids=true, to_apply=%region_32.33.clone | all-reduce | flops 9216 | bytes 73728
  1145.5 6.3 all-reduce.18
  1162.8 68.1 %all-reduce.23.cloned.1.call-done = (f32[96,768]{0,1:T(8,128)}, f32[96,768]{0,1:T(8,128)}, f32[96,768]{0,1:T(8,128)}, f32[96,768]{1,0:T(8,128)}, f32[96,3072]{1,0:T(8,128)}, /*index=5*/f32[384,768]{1,0:T(8,128)}) async-done(((f32[96,768]{0,1:T(8,128)}, f32[96,768]{0,1:T(8,128)}, f32[96,768]{0,1:T(8,128)}, f32[96,768]{1,0:T(8,128)}, f32[96,3072]{1,0:T(8,128)}, /*index=5*/f32[384,768]{1,0:T(8,128)}), ...) | async-done | bytes 3538960 | tf_op jit(solution)/shard_map/psum | solution.py:311
  (504 shorter events, 251.9 us)
Async XLA Ops:
  7.2 78.7 %copy-start.33 = (bf16[96,768]{1,0:T(8,128)(2,1)S(1)}, bf16[96,768]{1,0:T(8,128)(2,1)}, u32[]{:S(2)}) copy-start(bf16[96,768]{1,0:T(8,128)(2,1)} %param.30) | copy-start | bytes 442372
  7.2 91.5 %all-gather.8.cloned.1.call-start = ((), (), s32[]{:S(2)}) async-start(), calls=%async_computation.10 | async-start | bytes 1327104 | tf_op jit(solution)/shard_map/all_gather | solution.py:85
  7.9 93.6 %all-gather.10.cloned.1.call-start = ((), (), s32[]{:S(2)}) async-start(), calls=%async_computation.11 | async-start | bytes 1327104 | tf_op jit(solution)/shard_map/all_gather | solution.py:86
  8.7 215.2 %all-gather.12.cloned.1.call-start = ((), (), s32[]{:S(2)}) async-start(), calls=%async_computation.12 | async-start | bytes 1327104 | tf_op jit(solution)/shard_map/all_gather | solution.py:88
  9.4 218.4 %all-gather.14.cloned.1.call-start = ((), (), s32[]{:S(2)}) async-start(), calls=%async_computation.13 | async-start | bytes 5308416 | tf_op jit(solution)/shard_map/all_gather | solution.py:89
  10.0 10.1 collective-permute-start
  20.1 10.7 collective-permute-start.1
  20.1 10.9 collective-permute-start.4
  30.8 8.0 collective-permute-start.2
  31.0 54.7 %collective-permute-start.5 = (bf16[96,768]{1,0:T(8,128)(2,1)S(1)}, bf16[96,768]{1,0:T(8,128)(2,1)S(1)}, u32[]{:S(2)}, u32[]{:S(2)}) collective-permute-start(bf16[96,768]{1,0:T(8,128)(2,1)S(1)} %collective-permute-done.4), channel_id=1, source_target_pairs={{4,0},{8,4},{12,8},{16,12},{20,16},{24,20},{28,24},{0,28},{5,1},{9... | collective-permute-start | bytes 442376 | tf_op jit(solution)/shard_map/ppermute | solution.py:26
  38.8 47.1 %collective-permute-start.3 = (bf16[96,768]{1,0:T(8,128)(2,1)S(1)}, bf16[96,768]{1,0:T(8,128)(2,1)S(1)}, u32[]{:S(2)}, u32[]{:S(2)}) collective-permute-start(bf16[96,768]{1,0:T(8,128)(2,1)S(1)} %collective-permute-done.2), channel_id=1, source_target_pairs={{0,4},{4,8},{8,12},{12,16},{16,20},{20,24},{24,28},{28,0},{1,5},{5... | collective-permute-start | bytes 442376 | tf_op jit(solution)/shard_map/ppermute | solution.py:24
  85.8 8.3 collective-permute-start.6
  108.6 32.1 %all-to-all-start = ((bf16[3,2,256,768]{2,1,0,3:T(2,128)(2,1)}), bf16[3,2,256,768]{2,1,0,3:T(2,128)(2,1)S(1)}, u32[]{:S(2)}, u32[]{:S(2)}) async-start(bf16[3,2,256,768]{2,1,0,3:T(2,128)(2,1)} %pad_maximum_fusion), calls=%async_computation | async-start | bytes 4718592 | tf_op jit(solution)/shard_map/all_to_all | solution.py:120
  112.2 193.5 %all-gather.16.cloned.1.call-start = ((), (), s32[]{:S(2)}) async-start(), calls=%async_computation.14 | async-start | bytes 5308416 | tf_op jit(solution)/shard_map/all_gather | solution.py:90
  180.4 35.1 %copy-start.53 = (bf16[768]{0:T(1024)(128)(2,1)S(1)}, bf16[768]{0:T(1024)(128)(2,1)}, u32[]{:S(2)}) copy-start(bf16[768]{0:T(1024)(128)(2,1)} %get-tuple-element.499) | copy-start | bytes 4612
  183.9 39.9 %copy-start.22 = (bf16[2,256,768]{2,1,0:T(8,128)(2,1)S(1)}, bf16[2,256,768]{2,1,0:T(8,128)(2,1)}, u32[]{:S(2)}) copy-start(bf16[2,256,768]{2,1,0:T(8,128)(2,1)} %param.26) | copy-start | bytes 2359300
  183.9 31.6 %all-to-all-start.1 = ((bf16[2,1024,192]{2,0,1:T(2,128)(2,1)}), bf16[2,1024,192]{2,0,1:T(2,128)(2,1)}, u32[]{:S(2)}, u32[]{:S(2)}) async-start(bf16[2,1024,192]{2,0,1:T(2,128)(2,1)} %copy.115), calls=%async_computation.1 | async-start | bytes 2097152 | tf_op jit(solution)/shard_map/all_to_all | solution.py:162
  188.3 140.9 %copy-start.43 = (f32[768]{0:T(1024)}, f32[768]{0:T(1024)S(1)}, u32[]{:S(2)}) copy-start(f32[768]{0:T(1024)S(1)} %convert_element_type.183) | copy-start | bytes 9220
  188.4 117.4 %copy-start.49 = (f32[768]{0:T(1024)}, f32[768]{0:T(1024)S(1)}, u32[]{:S(2)}) copy-start(f32[768]{0:T(1024)S(1)} %convert_element_type.184) | copy-start | bytes 9220
  226.3 103.0 %copy-start.36 = (f32[512]{0:T(512)}, f32[512]{0:T(512)S(1)}, u32[]{:S(2)}) copy-start(f32[512]{0:T(512)S(1)} %broadcast_multiply_fusion.1) | copy-start | bytes 6148
  227.8 101.5 %copy-start.46 = (f32[512]{0:T(512)}, f32[512]{0:T(512)S(1)}, u32[]{:S(2)}) copy-start(f32[512]{0:T(512)S(1)} %fusion.51) | copy-start | bytes 6148
  334.6 15.1 %all-to-all-start.2 = ((bf16[2,256,768]{1,0,2:T(2,128)(2,1)}), bf16[2,256,768]{1,0,2:T(2,128)(2,1)S(1)}, u32[]{:S(2)}, u32[]{:S(2)}) async-start(bf16[2,256,768]{1,0,2:T(2,128)(2,1)} %copy.117), calls=%async_computation.2 | async-start | bytes 1572864 | tf_op jit(solution)/shard_map/all_to_all | solution.py:205
  338.1 220.1 %reduce-scatter.19.cloned.1.call-start = ((), (), s32[]{:S(2)}) async-start(), calls=%async_computation.19 | async-start | bytes 2654208
  491.7 138.2 %reduce-scatter.21.cloned.1.call-start = ((), (), s32[]{:S(2)}) async-start(), calls=%async_computation.20 | async-start | bytes 2654208
  500.6 201.1 %reduce-scatter.23.cloned.1.call-start = ((), (), s32[]{:S(2)}) async-start(), calls=%async_computation.21 | async-start | bytes 2654208
  508.7 264.7 %reduce-scatter.13.cloned.1.call-start = ((), (), s32[]{:S(2)}) async-start(), calls=%async_computation.16 | async-start | bytes 2654208 | tf_op jit(solution)/shard_map/reduce_scatter | solution.py:298
  512.4 427.1 %reduce-scatter.17.cloned.1.call-start = ((), (), s32[]{:S(2)}) async-start(), calls=%async_computation.18 | async-start | bytes 10616832 | tf_op jit(solution)/shard_map/reduce_scatter | solution.py:300
  520.9 584.8 %reduce-scatter.15.cloned.1.call-start = ((), (), s32[]{:S(2)}) async-start(), calls=%async_computation.17 | async-start | bytes 10616832 | tf_op jit(solution)/shard_map/reduce_scatter | solution.py:299
  530.6 628.3 %all-gather.18.cloned.1.call-start = ((), (), s32[]{:S(2)}) async-start(), calls=%async_computation.15 | async-start | bytes 1327104 | tf_op jit(solution)/shard_map/all_gather | solution.py:176
  531.1 699.7 %all-reduce.23.cloned.1.call-start = ((), (), s32[]{:S(2)}) async-start(), calls=%async_computation.22 | async-start | bytes 7667712 | tf_op jit(solution)/shard_map/psum | solution.py:311
  631.9 475.2 %copy-start.48 = (f32[2,256]{1,0:T(2,128)S(1)}, f32[2,256]{1,0:T(2,128)}, u32[]{:S(2)}) copy-start(f32[2,256]{1,0:T(2,128)} %get-tuple-element.530) | copy-start | bytes 6148
  1108.7 46.6 %copy-start.26 = (bf16[2,1,256,768]{3,2,0,1:T(8,128)(2,1)S(1)}, bf16[2,1,256,768]{3,2,0,1:T(8,128)(2,1)}, u32[]{:S(2)}) copy-start(bf16[2,1,256,768]{3,2,0,1:T(8,128)(2,1)} %copy.124) | copy-start | bytes 2359300
  (105 other events, 407.8 us)
Sparse Core Ops, SparseCore 0:
  10.2 48.4 all-gather.7
  60.9 40.5 all-gather.9
  103.7 40.9 all-gather.11
  146.7 78.8 all-gather.13
  227.7 78.0 all-gather.15
  491.9 66.3 reduce-scatter.18
  561.8 68.1 reduce-scatter.20
  633.5 68.1 reduce-scatter.22
  705.2 68.2 reduce-scatter.12
  776.9 162.5 reduce-scatter.16
  943.1 162.5 reduce-scatter.14
  1107.7 40.3 all-gather.17
  1151.5 79.3 all-reduce.22
